TPU v7x, 128 devices: a whole 4x4x4 slice. The times are simulated.
128 devices in a mesh: tm: 4 (over x), op: 32 (over y, z, core).
Axes of the slice: x: 4, y: 4, z: 4, core: 2. Of those that a mesh axis runs over, the one named last changes fastest.
Arguments:
- sink_elem: bfloat16 [2, 4, 2048, 16384], P(None, 'tm', 'op'), may hold values from -6 to 6
- source_elem: bfloat16 [2, 2, 2048, 16384], P(None, None, None, 'op'), may hold values from -6 to 6
- peram: bfloat16 [2, 4, 2, 512, 512], P(None, 'tm', None, 'op'), may hold values from -4 to 4
- pair_list: int32 [16, 1], replicated, may hold values from 0 to 15
- spin_sets: int32 [16, 3], replicated, may hold values from 0 to 3
Outputs:
- correlator: float32 [2, 4, 2, 16, 1], P(None, 'tm')
All inputs are finite; a program needn't handle non-finite values.
Results may differ from a plain program's by a relative error of at most 0.0041.
Values may be sent and summed in bfloat16 or wider, within the bound.
A program may use at most 192 MiB of HBM per device.

v0:
```python
import jax
import jax.numpy as jnp
from jax import lax
from jax.sharding import PartitionSpec as P

NEV = 128
NSPIN = 4
NOP = 16
TSRC = 2
PAIRS = 1


def complex_matrix(block):
    upper = jnp.concatenate([block[0], block[1]], axis=1)
    lower = jnp.concatenate([-block[1], block[0]], axis=1)
    return jnp.stack([upper, lower])


def on_device(sink_elem, source_elem, peram, pair_list, spin_sets):
    tau_all = lax.all_gather(peram, "op", axis=3, tiled=True)
    position = lax.axis_index("op")
    rows = sink_elem.shape[2]
    local_times = sink_elem.shape[1]
    span = min(rows, NEV)
    cols = source_elem.shape[3]

    def spin_block(local, t0, left, right):
        return lax.dynamic_slice(tau_all[:, local, t0], (0, left * NEV, right * NEV), (2, NEV, NEV))

    def sink_side(local, t0, p):
        op_now = (position * rows + 0) // NEV
        mine = spin_sets[op_now]
        theirs = spin_sets[pair_list[op_now, p]]
        third = complex_matrix(spin_block(local, t0, mine[2], theirs[2]))
        second = complex_matrix(spin_block(local, t0, mine[1], theirs[1]))
        phi = sink_elem[:, local, 0:span].reshape(2, span * NEV, NEV)
        x_both = jnp.einsum("cxk,ckb->xb", phi, third, preferred_element_type=jnp.float32)
        x_both = x_both.astype(jnp.bfloat16).reshape(span, NEV, 2, NEV)
        y_both = jnp.einsum("ijck,cjb->ibk", x_both, second, preferred_element_type=jnp.float32)
        y_both = y_both.astype(jnp.bfloat16).reshape(span, 2, NEV * NEV)
        pieces = jnp.transpose(y_both, (1, 0, 2))
        return pieces

    partial_terms = {}
    combos = [
        (local, t0, p) for local in range(local_times) for t0 in range(TSRC) for p in range(PAIRS)
    ]
    stacked = jnp.stack([sink_side(local, t0, p) for local, t0, p in combos], axis=1)
    columns = lax.all_to_all(stacked, "op", split_axis=3, concat_axis=2, tiled=True)
    for index, combo in enumerate(combos):
        column_t0 = combo[1]
        other = pair_list[:, combo[2]]
        source = source_elem[:, column_t0].reshape(2, NOP, NEV, cols)
        chosen = jnp.take(source, other, axis=1)
        tiles = columns[:, index].reshape(2, NOP, NEV, cols)

        def inner(a, b):
            return jnp.einsum("oic,ojc->oij", a, b, preferred_element_type=jnp.float32)

        m_re = inner(tiles[0], chosen[0]) + inner(tiles[1], chosen[1])
        m_im = inner(tiles[1], chosen[0]) - inner(tiles[0], chosen[1])
        blocks = tau_all[:, combo[0], column_t0].reshape(2, NSPIN, NEV, NSPIN, NEV)
        blocks = jnp.transpose(blocks, (1, 3, 0, 2, 4))
        first = blocks[spin_sets[:, 0], spin_sets[other, 0]].astype(jnp.float32)
        c_re = jnp.sum(first[:, 0] * m_re - first[:, 1] * m_im, axis=(1, 2))
        c_im = jnp.sum(first[:, 0] * m_im + first[:, 1] * m_re, axis=(1, 2))
        partial_terms[combo] = jnp.stack([c_re, c_im])
    local = 0
    per_time = []
    for t0 in range(TSRC):
        per_time.append(jnp.stack([partial_terms[local, t0, 0]], axis=-1))
    per_local = [jnp.stack(per_time, axis=1)]
    partial_sum = jnp.stack(per_local, axis=1)
    totals = lax.psum(partial_sum, "op")
    return totals * (1.0 / float(NEV**3))


def solution(mesh):
    in_specs = (
        P(None, "tm", "op", None),
        P(None, None, None, "op"),
        P(None, "tm", None, "op", None),
        P(),
        P(),
    )
    out_specs = P(None, "tm", None, None, None)
    return jax.shard_map(
        on_device, mesh=mesh, in_specs=in_specs, out_specs=out_specs, check_vma=False
    )
```

profile of v0, /device:TPU:1, one launch (start us, length us, event | category | flops | bytes accessed | tf_op | source)
XLA Modules:
  0.0 462.1 jit_solution(5356037397111504323)
XLA Ops:
  6.5 1.5 copy.40
  8.1 1.2 constant_dynamic-slice_fusion.1
  11.3 0.8 constant_dynamic-slice_fusion
  15.2 7.4 %reshape_squeeze.19 = bf16[2,8192,128]{2,1,0:T(8,128)(2,1)} reshape(bf16[2,1,64,16384]{3,2,1,0:T(8,128)(2,1)} %param.7) | data formatting | bytes 8388608 | tf_op jit(solution)/shard_map/reshape;squeeze | solution.py:36
  22.6 34.7 %all-gather.2.cloned.1.call-done = bf16[2,1,2,512,512]{4,2,1,0,3:T(2,128)(2,1)} async-done(((bf16[2,1,2,16,512]{4,2,1,0,3:T(2,128)(2,1)}), bf16[2,1,2,512,512]{4,2,1,0,3:T(2,128)(2,1)}) %all-gather.2.cloned.1.call-update) | async-done | bytes 2097168 | tf_op jit(solution)/shard_map/all_gather | solution.py:20
  57.3 6.5 %fusion.57 = (bf16[2,1,1,512,512]{4,2,1,0,3:T(2,128)(2,1)}, bf16[2,1,1,512,512]{4,2,1,0,3:T(2,128)(2,1)S(1)}) fusion(bf16[2,1,2,512,512]{4,2,1,0,3:T(2,128)(2,1)} %all-gather.2.cloned.1.call-done), kind=kLoop, calls=%fused_computation.113 | loop fusion | bytes 4194304 | tf_op jit(solution)/shard_map/slice | solution.py:62
  63.8 4.6 copy.59
  68.4 4.2 copy.60
  72.6 0.8 dynamic-slice_bitcast_fusion.3
  73.4 0.8 fusion.53
  74.2 3.5 fusion.15
  77.7 1.2 copy.61
  78.9 7.4 %fusion.2 = bf16[64,256,128]{2,1,0:T(8,128)(2,1)} fusion(bf16[64,128,2,128]{1,0,3,2:T(8,128)(2,1)S(1)} %bitcast.218, bf16[1,128,256]{1,2,0:T(8,128)(2,1)S(1)} %get-tuple-element.35, bf16[1,128,256]{1,2,0:T(8,128)(2,1)S(1)} %get-tuple-element.34), kind=kOutput, calls=%fused_computation.12 | convolution fusion | flops 1076101120 | bytes 8519680 | tf_op jit(solution)/shard_map/ijck,cjb->ibk/dot_general | solution.py:39
  86.4 6.9 %reshape.75 = bf16[64,2,16384]{2,1,0:T(2,128)(2,1)} reshape(bf16[64,256,128]{2,1,0:T(8,128)(2,1)} %fusion.2) | data formatting | bytes 8388608 | tf_op jit(solution)/shard_map/reshape | solution.py:40
  93.2 6.6 %copy.83 = bf16[64,2,16384]{2,0,1:T(8,128)(2,1)} copy(bf16[64,2,16384]{2,1,0:T(2,128)(2,1)} %reshape.75) | data formatting | bytes 8388608 | tf_op jit(solution)/shard_map/reshape | solution.py:40
  99.9 1.3 fusion.14
  101.2 1.2 copy.62
  102.4 7.4 %fusion.3 = bf16[64,256,128]{2,1,0:T(8,128)(2,1)} fusion(bf16[64,128,2,128]{1,0,3,2:T(8,128)(2,1)S(1)} %bitcast.219, bf16[1,128,256]{1,2,0:T(8,128)(2,1)S(1)} %get-tuple-element.39, bf16[1,128,256]{1,2,0:T(8,128)(2,1)S(1)} %get-tuple-element.38), kind=kOutput, calls=%fused_computation.13 | convolution fusion | flops 1076101120 | bytes 8519680 | tf_op jit(solution)/shard_map/ijck,cjb->ibk/dot_general | solution.py:39
  109.8 6.9 %reshape.77 = bf16[64,2,16384]{2,1,0:T(2,128)(2,1)} reshape(bf16[64,256,128]{2,1,0:T(8,128)(2,1)} %fusion.3) | data formatting | bytes 8388608 | tf_op jit(solution)/shard_map/reshape | solution.py:40
  116.7 6.6 %copy.82 = bf16[64,2,16384]{2,0,1:T(8,128)(2,1)} copy(bf16[64,2,16384]{2,1,0:T(2,128)(2,1)} %reshape.77) | data formatting | bytes 8388608 | tf_op jit(solution)/shard_map/reshape | solution.py:40
  123.3 6.2 %pad_maximum_fusion = bf16[2,2,64,16384]{3,2,1,0:T(8,128)(2,1)} fusion(bf16[2,1,64,16384]{3,2,1,0:T(8,128)(2,1)} %bitcast.222, bf16[2,1,64,16384]{3,2,1,0:T(8,128)(2,1)S(1)} %bitcast.220), kind=kLoop, calls=%fused_computation.9 | loop fusion | flops 4194304 | bytes 16777216 | tf_op jit(solution)/shard_map/stack | solution.py:48
  129.5 34.5 %copy.49 = bf16[2,2,64,16384]{2,1,0,3:T(2,128)(2,1)} copy(bf16[2,2,64,16384]{3,2,1,0:T(8,128)(2,1)} %pad_maximum_fusion) | data formatting | bytes 16777216 | tf_op jit(solution)/shard_map/stack | solution.py:48
  164.0 26.7 %reshape.124 = bf16[32,2,65536]{2,1,0:T(2,128)(2,1)} reshape(bf16[16384,2,2,64]{3,2,1,0:T(2,128)(2,1)} %bitcast.211) | data formatting | bytes 16777216
  190.7 5.4 %all-to-all-start = ((bf16[32,2,65536]{2,1,0:T(2,128)(2,1)}), bf16[32,2,65536]{2,1,0:T(2,128)(2,1)}, u32[]{:S(2)}, u32[]{:S(2)}) async-start(bf16[32,2,65536]{2,1,0:T(2,128)(2,1)} %reshape.124), calls=%async_computation | async-start | bytes 16777216 | tf_op jit(solution)/shard_map/all_to_all | solution.py:49
  196.2 5.8 %fusion.56 = (bf16[2,1,2048,512]{3,2,1,0:T(8,128)(2,1)}, bf16[2,1,2048,512]{3,2,1,0:T(8,128)(2,1)}) fusion(bf16[2,2,2048,512]{3,2,1,0:T(8,128)(2,1)} %param.8), kind=kLoop, calls=%fused_computation.112 | loop fusion | bytes 16777216 | tf_op jit(solution)/shard_map/slice | solution.py:53
  202.0 5.0 %gather_fusion.3 = bf16[16,2,128,512]{3,2,1,0:T(8,128)(2,1)} fusion(bf16[2,16,128,512]{3,2,1,0:T(8,128)(2,1)} %bitcast.223, s32[1024]{0:T(1024)S(1)} %pad_clamp_fusion), kind=kCustom, calls=%fused_computation.clone | custom fusion | bytes 8388672 | tf_op jit(solution)/shard_map/jit(_take)/gather | solution.py:54
  207.0 5.0 %gather_fusion.4 = bf16[16,2,128,512]{3,2,1,0:T(8,128)(2,1)} fusion(bf16[2,16,128,512]{3,2,1,0:T(8,128)(2,1)} %bitcast.221, s32[1024]{0:T(1024)S(1)} %pad_clamp_fusion), kind=kCustom, calls=%fused_computation.1.clone | custom fusion | bytes 8388672 | tf_op jit(solution)/shard_map/jit(_take)/gather | solution.py:54
  212.7 6.0 %fusion.5 = (bf16[2,16,128,512]{3,2,1,0:T(8,128)(2,1)}, bf16[2,16,128,512]{3,2,1,0:T(8,128)(2,1)}) fusion(bf16[16,2,128,512]{3,2,1,0:T(8,128)(2,1)} %gather_fusion.3, pred[16]{0:T(512)(128)(4,1)S(1)} %compare_and_fusion, bf16[16,2,128,512]{3,2,1,0:T(8,128)(2,1)} %gather_fusion.4), kind=kLoop, calls=%fused_computation.17 | loop fusion | flops 4194304 | bytes 16777232 | tf_op jit(solution)/shard_map/jit(_take)/select_n | solution.py:54
  218.9 1.1 reshape_squeeze.21
  220.1 1.5 copy.42
  221.6 1.7 copy.52
  223.3 2.0 gather_fusion.1
  225.3 0.8 gather_fusion.2
  226.0 1.5 copy_convert_fusion.1
  227.6 1.6 copy_convert_fusion
  229.2 75.5 %all-to-all-done = bf16[32,2,65536]{2,1,0:T(2,128)(2,1)} async-done(((bf16[32,2,65536]{2,1,0:T(2,128)(2,1)}), bf16[32,2,65536]{2,1,0:T(2,128)(2,1)}, u32[]{:S(2)}, u32[]{:S(2)}) %all-to-all-start) | async-done | bytes 8388640 | tf_op jit(solution)/shard_map/all_to_all | solution.py:49
  304.7 26.0 %reshape.125 = bf16[16384,2,2,64]{3,2,1,0:T(2,128)(2,1)} reshape(bf16[32,2,65536]{2,1,0:T(2,128)(2,1)} %all-to-all-done) | data formatting | bytes 16777216
  330.7 36.1 %copy.50 = bf16[2,2,32,64,512]{4,3,2,1,0:T(8,128)(2,1)} copy(bf16[2,2,32,64,512]{3,1,0,4,2:T(2,128)(2,1)} %bitcast.212) | data formatting | bytes 16777216 | tf_op jit(solution)/shard_map/all_to_all | solution.py:49
  366.8 4.0 fusion.55
  372.1 0.7 fusion.16
  372.9 0.8 fusion.26
  373.6 1.4 copy-done.2
  376.5 0.7 fusion.24
  377.2 0.9 copy-done.7
  378.0 0.8 subtract_reduce_fusion.1
  378.9 0.7 copy-done.6
  379.6 0.8 subtract_reduce_fusion
  380.5 74.2 %psum.7 = f32[2,1,2,16,1]{3,2,0,4,1:T(2,128)S(1)} all-reduce(f32[2,1,2,16,1]{3,2,0,4,1:T(2,128)S(1)} %bitcast.230), channel_id=1, replica_groups=mesh['tm'=4,'op'=32] {'op'}, use_global_device_ids=true, to_apply=%region_4.6 | all-reduce | flops 64 | bytes 512 | tf_op jit(solution)/shard_map/psum | solution.py:74
  (39 shorter events, 5.1 us)
Async XLA Ops:
  6.5 50.8 %all-gather.2.cloned.1.call-start = ((), (), s32[]{:S(2)}) async-start(), calls=%async_computation.1 | async-start | bytes 2162688 | tf_op jit(solution)/shard_map/all_gather | solution.py:20
  93.2 6.6 %copy-start.1 = (bf16[2,8192,128]{2,1,0:T(8,128)(2,1)S(1)}, bf16[2,8192,128]{2,1,0:T(8,128)(2,1)}, u32[]{:S(2)}) copy-start(bf16[2,8192,128]{2,1,0:T(8,128)(2,1)} %reshape_squeeze.19) | copy-start | bytes 12582916
  116.7 6.6 %copy-start.4 = (bf16[64,2,16384]{2,0,1:T(8,128)(2,1)S(1)}, bf16[64,2,16384]{2,0,1:T(8,128)(2,1)}, u32[]{:S(2)}) copy-start(bf16[64,2,16384]{2,0,1:T(8,128)(2,1)} %copy.83) | copy-start | bytes 12582916
  190.7 5.4 %copy-start.8 = (s32[16,1]{0,1:T(1,128)S(1)}, s32[16,1]{0,1:T(1,128)}, u32[]{:S(2)}) copy-start(s32[16,1]{0,1:T(1,128)} %param.10) | copy-start | bytes 196
  190.7 114.0 %all-to-all-start = ((bf16[32,2,65536]{2,1,0:T(2,128)(2,1)}), bf16[32,2,65536]{2,1,0:T(2,128)(2,1)}, u32[]{:S(2)}, u32[]{:S(2)}) async-start(bf16[32,2,65536]{2,1,0:T(2,128)(2,1)} %reshape.124), calls=%async_computation | async-start | bytes 16777216 | tf_op jit(solution)/shard_map/all_to_all | solution.py:49
  207.0 5.0 %copy-start = (s32[16,3]{0,1:T(4,128)S(1)}, s32[16,3]{0,1:T(4,128)}, u32[]{:S(2)}) copy-start(s32[16,3]{0,1:T(4,128)} %param.11) | copy-start | bytes 580
  212.7 6.3 %copy-start.5 = (bf16[2,1,1,512,512]{3,4,2,1,0:T(8,128)(2,1)S(1)}, bf16[2,1,1,512,512]{3,4,2,1,0:T(8,128)(2,1)}, u32[]{:S(2)}) copy-start(bf16[2,1,1,512,512]{3,4,2,1,0:T(8,128)(2,1)} %copy.60) | copy-start | bytes 3145732
  366.8 4.7 %copy-start.3 = (bf16[2,16,128,512]{3,2,1,0:T(8,128)(2,1)S(1)}, bf16[2,16,128,512]{3,2,1,0:T(8,128)(2,1)}, u32[]{:S(2)}) copy-start(bf16[2,16,128,512]{3,2,1,0:T(8,128)(2,1)} %get-tuple-element.48) | copy-start | bytes 12582916
  372.8 2.2 copy-start.2
  376.5 1.6 copy-start.7
  378.0 1.6 copy-start.6
Sparse Core Ops, SparseCore 0:
  9.6 47.6 all-gather.1
where the time goes:
time: 467 us; the launch traced here: 462 us
  local copies, waits for them, and re-layouts  212 us (45%)
  waiting for transfers between devices  110 us (24%)
  blocking collectives  74.2 us (16%)
  matrix products  25.6 us (5%)
  between operations  18.1 us (4%)
  other arithmetic  16.8 us (4%)
  starting transfers between devices  5.43 us (1%)
    all_to_all x1, waiting for transfers between devices, on_device(): lax.all_to_all(stacked, 'op', split_axis=3, concat_axis=2, tiled=True)  75.5 us
    psum x1, blocking collectives, on_device(): totals = lax.psum(partial_sum, 'op')  74.2 us
    unnamed x25, local copies, waits for them, and re-layouts  69.1 us
    all_to_all x1, local copies, waits for them, and re-layouts, on_device(): lax.all_to_all(stacked, 'op', split_axis=3, concat_axis=2, tiled=True)  36.1 us
    all_gather x1, waiting for transfers between devices, on_device(): tau_all = lax.all_gather(peram, 'op', axis=3, tiled=True)  34.7 us
    another operation x1, local copies, waits for them, and re-layouts, on_device(): jnp.stack([sink_side(local, t0, p) for local, t0, p in combos], axis=1)  34.5 us
    reshape x4, local copies, waits for them, and re-layouts, sink_side(): y_both = y_both.astype(jnp.bfloat16).reshape(span, 2, NEV * NEV)  27 us
    dot_general x2, matrix products, sink_side(): jnp.einsum('ijck,cjb->ibk', x_both, second, preferred_element_type=jnp.fl...  14.9 us
  transfers between devices with their start and end apart: 2, of which 2 were waited for; matrix products, arithmetic and copies ran while one was open for 9% of the time, Pallas kernels for 0%

commit v1 on v0

--- a/solution.py
+++ b/solution.py
@@ -8,6 +8,12 @@
 NOP = 16
 TSRC = 2
 PAIRS = 1
+
+
+def summed_here(x, axis):
+    parts = lax.all_gather(x, axis, axis=0, tiled=False)
+    total = parts.sum(axis=0)
+    return total
 
 
 def complex_matrix(block):
@@ -71,7 +77,7 @@
         per_time.append(jnp.stack([partial_terms[local, t0, 0]], axis=-1))
     per_local = [jnp.stack(per_time, axis=1)]
     partial_sum = jnp.stack(per_local, axis=1)
-    totals = lax.psum(partial_sum, "op")
+    totals = summed_here(partial_sum, "op")
     return totals * (1.0 / float(NEV**3))
 
 

time: 467 us -> 431 us (0.923)
  blocking collectives: 74.2 us -> 38.8 us
    psum x1 -> x0, blocking collectives: 74.2 us -> none  [on_device(): totals = lax.psum(partial_sum, 'op')]
    all_gather x0 -> x1, blocking collectives: none -> 38.8 us  [summed_here(): parts = lax.all_gather(x, axis, axis=0, tiled=False)]
  transfers between devices with their start and end apart: 2 -> 2, of which waited for: 2 -> 2; matrix products, arithmetic and copies ran while one was open for 9% -> 10% of each run, Pallas kernels for 0% -> 0%
where the time goes in v1:
time: 431 us; the launch traced here: 427 us
  local copies, waits for them, and re-layouts  212 us (49%)
  waiting for transfers between devices  110 us (26%)
  blocking collectives  38.8 us (9%)
  matrix products  25.6 us (6%)
  between operations  18.1 us (4%)
  other arithmetic  16.3 us (4%)
  starting transfers between devices  5.43 us (1%)
    all_to_all x1, waiting for transfers between devices, on_device(): lax.all_to_all(stacked, 'op', split_axis=3, concat_axis=2, tiled=True)  75.5 us
    unnamed x25, local copies, waits for them, and re-layouts  69.1 us
    all_gather x1, blocking collectives, summed_here(): parts = lax.all_gather(x, axis, axis=0, tiled=False)  38.8 us
    all_to_all x1, local copies, waits for them, and re-layouts, on_device(): lax.all_to_all(stacked, 'op', split_axis=3, concat_axis=2, tiled=True)  36.1 us
    all_gather x1, waiting for transfers between devices, on_device(): tau_all = lax.all_gather(peram, 'op', axis=3, tiled=True)  34.7 us
    another operation x1, local copies, waits for them, and re-layouts, on_device(): jnp.stack([sink_side(local, t0, p) for local, t0, p in combos], axis=1)  34.5 us
    reshape x4, local copies, waits for them, and re-layouts, sink_side(): y_both = y_both.astype(jnp.bfloat16).reshape(span, 2, NEV * NEV)  27 us
    dot_general x2, matrix products, sink_side(): jnp.einsum('ijck,cjb->ibk', x_both, second, preferred_element_type=jnp.fl...  14.9 us
  transfers between devices with their start and end apart: 2, of which 2 were waited for; matrix products, arithmetic and copies ran while one was open for 10% of the time, Pallas kernels for 0%

profile of v1, /device:TPU:1, one launch (start us, length us, event | category | flops | bytes accessed | tf_op | source)
XLA Modules:
  0.0 426.8 jit_solution(5722338821308368324)
XLA Ops:
  6.5 1.5 copy.40
  8.1 1.2 constant_dynamic-slice_fusion.1
  11.3 0.8 constant_dynamic-slice_fusion
  15.2 7.4 %reshape_squeeze.19 = bf16[2,8192,128]{2,1,0:T(8,128)(2,1)} reshape(bf16[2,1,64,16384]{3,2,1,0:T(8,128)(2,1)} %param.7) | data formatting | bytes 8388608 | tf_op jit(solution)/shard_map/reshape;squeeze | solution.py:42
  22.6 34.7 %all-gather.3.cloned.1.call-done = bf16[2,1,2,512,512]{4,2,1,0,3:T(2,128)(2,1)} async-done(((bf16[2,1,2,16,512]{4,2,1,0,3:T(2,128)(2,1)}), bf16[2,1,2,512,512]{4,2,1,0,3:T(2,128)(2,1)}) %all-gather.3.cloned.1.call-update) | async-done | bytes 2097168 | tf_op jit(solution)/shard_map/all_gather | solution.py:26
  57.3 6.5 %fusion.58 = (bf16[2,1,1,512,512]{4,2,1,0,3:T(2,128)(2,1)}, bf16[2,1,1,512,512]{4,2,1,0,3:T(2,128)(2,1)S(1)}) fusion(bf16[2,1,2,512,512]{4,2,1,0,3:T(2,128)(2,1)} %all-gather.3.cloned.1.call-done), kind=kLoop, calls=%fused_computation.113 | loop fusion | bytes 4194304 | tf_op jit(solution)/shard_map/slice | solution.py:68
  63.8 4.6 %copy.64 = bf16[2,1,1,512,512]{3,4,2,1,0:T(8,128)(2,1)S(1)} copy(bf16[2,1,1,512,512]{4,2,1,0,3:T(2,128)(2,1)} %get-tuple-element.24) | data formatting | bytes 2097152
  68.4 4.2 copy.65
  72.6 0.8 dynamic-slice_bitcast_fusion.3
  73.4 0.8 fusion.54
  74.2 3.5 fusion.15
  77.7 1.2 copy.66
  78.9 7.4 %fusion.2 = bf16[64,256,128]{2,1,0:T(8,128)(2,1)} fusion(bf16[64,128,2,128]{1,0,3,2:T(8,128)(2,1)S(1)} %bitcast.217, bf16[1,128,256]{1,2,0:T(8,128)(2,1)S(1)} %get-tuple-element.35, bf16[1,128,256]{1,2,0:T(8,128)(2,1)S(1)} %get-tuple-element.34), kind=kOutput, calls=%fused_computation.12 | convolution fusion | flops 1076101120 | bytes 8519680 | tf_op jit(solution)/shard_map/ijck,cjb->ibk/dot_general | solution.py:45
  86.4 6.9 %reshape.86 = bf16[64,2,16384]{2,1,0:T(2,128)(2,1)} reshape(bf16[64,256,128]{2,1,0:T(8,128)(2,1)} %fusion.2) | data formatting | bytes 8388608 | tf_op jit(solution)/shard_map/reshape | solution.py:46
  93.2 6.6 %copy.90 = bf16[64,2,16384]{2,0,1:T(8,128)(2,1)} copy(bf16[64,2,16384]{2,1,0:T(2,128)(2,1)} %reshape.86) | data formatting | bytes 8388608 | tf_op jit(solution)/shard_map/reshape | solution.py:46
  99.9 1.3 fusion.14
  101.2 1.2 copy.67
  102.4 7.4 %fusion.3 = bf16[64,256,128]{2,1,0:T(8,128)(2,1)} fusion(bf16[64,128,2,128]{1,0,3,2:T(8,128)(2,1)S(1)} %bitcast.218, bf16[1,128,256]{1,2,0:T(8,128)(2,1)S(1)} %get-tuple-element.39, bf16[1,128,256]{1,2,0:T(8,128)(2,1)S(1)} %get-tuple-element.38), kind=kOutput, calls=%fused_computation.13 | convolution fusion | flops 1076101120 | bytes 8519680 | tf_op jit(solution)/shard_map/ijck,cjb->ibk/dot_general | solution.py:45
  109.8 6.9 %reshape.88 = bf16[64,2,16384]{2,1,0:T(2,128)(2,1)} reshape(bf16[64,256,128]{2,1,0:T(8,128)(2,1)} %fusion.3) | data formatting | bytes 8388608 | tf_op jit(solution)/shard_map/reshape | solution.py:46
  116.7 6.6 %copy.89 = bf16[64,2,16384]{2,0,1:T(8,128)(2,1)} copy(bf16[64,2,16384]{2,1,0:T(2,128)(2,1)} %reshape.88) | data formatting | bytes 8388608 | tf_op jit(solution)/shard_map/reshape | solution.py:46
  123.3 6.2 %pad_maximum_fusion = bf16[2,2,64,16384]{3,2,1,0:T(8,128)(2,1)} fusion(bf16[2,1,64,16384]{3,2,1,0:T(8,128)(2,1)} %bitcast.221, bf16[2,1,64,16384]{3,2,1,0:T(8,128)(2,1)S(1)} %bitcast.219), kind=kLoop, calls=%fused_computation.9 | loop fusion | flops 4194304 | bytes 16777216 | tf_op jit(solution)/shard_map/stack | solution.py:54
  129.5 34.5 %copy.49 = bf16[2,2,64,16384]{2,1,0,3:T(2,128)(2,1)} copy(bf16[2,2,64,16384]{3,2,1,0:T(8,128)(2,1)} %pad_maximum_fusion) | data formatting | bytes 16777216 | tf_op jit(solution)/shard_map/stack | solution.py:54
  164.0 26.7 %reshape.137 = bf16[32,2,65536]{2,1,0:T(2,128)(2,1)} reshape(bf16[16384,2,2,64]{3,2,1,0:T(2,128)(2,1)} %bitcast.210) | data formatting | bytes 16777216
  190.7 5.4 %all-to-all-start = ((bf16[32,2,65536]{2,1,0:T(2,128)(2,1)}), bf16[32,2,65536]{2,1,0:T(2,128)(2,1)}, u32[]{:S(2)}, u32[]{:S(2)}) async-start(bf16[32,2,65536]{2,1,0:T(2,128)(2,1)} %reshape.137), calls=%async_computation | async-start | bytes 16777216 | tf_op jit(solution)/shard_map/all_to_all | solution.py:55
  196.2 5.8 %fusion.57 = (bf16[2,1,2048,512]{3,2,1,0:T(8,128)(2,1)}, bf16[2,1,2048,512]{3,2,1,0:T(8,128)(2,1)}) fusion(bf16[2,2,2048,512]{3,2,1,0:T(8,128)(2,1)} %param.8), kind=kLoop, calls=%fused_computation.112 | loop fusion | bytes 16777216 | tf_op jit(solution)/shard_map/slice | solution.py:59
  202.0 5.0 %gather_fusion.3 = bf16[16,2,128,512]{3,2,1,0:T(8,128)(2,1)} fusion(bf16[2,16,128,512]{3,2,1,0:T(8,128)(2,1)} %bitcast.222, s32[1024]{0:T(1024)S(1)} %pad_clamp_fusion), kind=kCustom, calls=%fused_computation.clone | custom fusion | bytes 8388672 | tf_op jit(solution)/shard_map/jit(_take)/gather | solution.py:60
  207.0 5.0 %gather_fusion.4 = bf16[16,2,128,512]{3,2,1,0:T(8,128)(2,1)} fusion(bf16[2,16,128,512]{3,2,1,0:T(8,128)(2,1)} %bitcast.220, s32[1024]{0:T(1024)S(1)} %pad_clamp_fusion), kind=kCustom, calls=%fused_computation.1.clone | custom fusion | bytes 8388672 | tf_op jit(solution)/shard_map/jit(_take)/gather | solution.py:60
  212.7 6.0 %fusion.5 = (bf16[2,16,128,512]{3,2,1,0:T(8,128)(2,1)}, bf16[2,16,128,512]{3,2,1,0:T(8,128)(2,1)}) fusion(bf16[16,2,128,512]{3,2,1,0:T(8,128)(2,1)} %gather_fusion.3, pred[16]{0:T(512)(128)(4,1)S(1)} %compare_and_fusion, bf16[16,2,128,512]{3,2,1,0:T(8,128)(2,1)} %gather_fusion.4), kind=kLoop, calls=%fused_computation.17 | loop fusion | flops 4194304 | bytes 16777232 | tf_op jit(solution)/shard_map/jit(_take)/select_n | solution.py:60
  218.9 1.1 reshape_squeeze.21
  220.1 1.5 copy.42
  221.6 1.7 copy.52
  223.3 2.0 gather_fusion.1
  225.3 0.8 gather_fusion.2
  226.0 1.5 copy_convert_fusion.1
  227.6 1.6 copy_convert_fusion
  229.2 75.5 %all-to-all-done = bf16[32,2,65536]{2,1,0:T(2,128)(2,1)} async-done(((bf16[32,2,65536]{2,1,0:T(2,128)(2,1)}), bf16[32,2,65536]{2,1,0:T(2,128)(2,1)}, u32[]{:S(2)}, u32[]{:S(2)}) %all-to-all-start) | async-done | bytes 8388640 | tf_op jit(solution)/shard_map/all_to_all | solution.py:55
  304.7 26.0 %reshape.138 = bf16[16384,2,2,64]{3,2,1,0:T(2,128)(2,1)} reshape(bf16[32,2,65536]{2,1,0:T(2,128)(2,1)} %all-to-all-done) | data formatting | bytes 16777216
  330.7 36.1 %copy.50 = bf16[2,2,32,64,512]{4,3,2,1,0:T(8,128)(2,1)} copy(bf16[2,2,32,64,512]{3,1,0,4,2:T(2,128)(2,1)} %bitcast.211) | data formatting | bytes 16777216 | tf_op jit(solution)/shard_map/all_to_all | solution.py:55
  366.8 4.0 fusion.56
  372.1 0.7 fusion.16
  372.9 0.8 fusion.26
  373.6 1.4 copy-done.2
  376.5 0.7 fusion.24
  377.2 0.9 copy-done.7
  378.0 0.8 subtract_reduce_fusion.1
  378.9 0.7 copy-done.6
  379.6 0.8 subtract_reduce_fusion
  380.5 38.8 %all-gather = f32[64,2,16,1]{2,1,3,0:T(2,128)S(1)} all-gather(f32[2,2,16,1]{2,1,3,0:T(2,128)S(1)} %copy.55), channel_id=2, replica_groups=mesh['tm'=4,'op'=32] {'op'}, dimensions={0}, use_global_device_ids=true | all-gather | bytes 8448 | tf_op jit(solution)/shard_map/all_gather | solution.py:14
  (41 shorter events, 5.2 us)
Async XLA Ops:
  6.5 50.8 %all-gather.3.cloned.1.call-start = ((), (), s32[]{:S(2)}) async-start(), calls=%async_computation.1 | async-start | bytes 2162688 | tf_op jit(solution)/shard_map/all_gather | solution.py:26
  93.2 6.6 %copy-start.1 = (bf16[2,8192,128]{2,1,0:T(8,128)(2,1)S(1)}, bf16[2,8192,128]{2,1,0:T(8,128)(2,1)}, u32[]{:S(2)}) copy-start(bf16[2,8192,128]{2,1,0:T(8,128)(2,1)} %reshape_squeeze.19) | copy-start | bytes 12582916
  116.7 6.6 %copy-start.4 = (bf16[64,2,16384]{2,0,1:T(8,128)(2,1)S(1)}, bf16[64,2,16384]{2,0,1:T(8,128)(2,1)}, u32[]{:S(2)}) copy-start(bf16[64,2,16384]{2,0,1:T(8,128)(2,1)} %copy.90) | copy-start | bytes 12582916
  190.7 5.4 %copy-start.8 = (s32[16,1]{0,1:T(1,128)S(1)}, s32[16,1]{0,1:T(1,128)}, u32[]{:S(2)}) copy-start(s32[16,1]{0,1:T(1,128)} %param.10) | copy-start | bytes 196
  190.7 114.0 %all-to-all-start = ((bf16[32,2,65536]{2,1,0:T(2,128)(2,1)}), bf16[32,2,65536]{2,1,0:T(2,128)(2,1)}, u32[]{:S(2)}, u32[]{:S(2)}) async-start(bf16[32,2,65536]{2,1,0:T(2,128)(2,1)} %reshape.137), calls=%async_computation | async-start | bytes 16777216 | tf_op jit(solution)/shard_map/all_to_all | solution.py:55
  207.0 5.0 %copy-start = (s32[16,3]{0,1:T(4,128)S(1)}, s32[16,3]{0,1:T(4,128)}, u32[]{:S(2)}) copy-start(s32[16,3]{0,1:T(4,128)} %param.11) | copy-start | bytes 580
  212.7 6.3 %copy-start.5 = (bf16[2,1,1,512,512]{3,4,2,1,0:T(8,128)(2,1)S(1)}, bf16[2,1,1,512,512]{3,4,2,1,0:T(8,128)(2,1)}, u32[]{:S(2)}) copy-start(bf16[2,1,1,512,512]{3,4,2,1,0:T(8,128)(2,1)} %copy.65) | copy-start | bytes 3145732
  366.8 4.7 %copy-start.3 = (bf16[2,16,128,512]{3,2,1,0:T(8,128)(2,1)S(1)}, bf16[2,16,128,512]{3,2,1,0:T(8,128)(2,1)}, u32[]{:S(2)}) copy-start(bf16[2,16,128,512]{3,2,1,0:T(8,128)(2,1)} %get-tuple-element.48) | copy-start | bytes 12582916
  372.8 2.2 copy-start.2
  376.5 1.6 copy-start.7
  378.0 1.6 copy-start.6
Sparse Core Ops, SparseCore 0:
  9.6 47.6 all-gather.2
